TPU v7x, 256 devices: a whole 4x4x8 slice. The times are simulated.
256 devices in a mesh: region: 32 (over y, z), sub: 8 (over x, core).
Axes of the slice: x: 4, y: 4, z: 8, core: 2. Of those that a mesh axis runs over, the one named last changes fastest.
Arguments:
- mode_rows: bfloat16 [131072, 4096], P(('region', 'sub')), may hold values from -0.09375 to 0.09375
- input_rows: bfloat16 [512, 4096], P(('region', 'sub')), may hold values from -0.25 to 0.25
- input_factor: bfloat16 [512, 128], P(('region', 'sub')), may hold values from -6 to 6
- mode_freq: float32 [4096], replicated, may hold values from 0.5 to 2
- mode_damping: float32 [4096], replicated, may hold values from 0.02 to 0.2
- line_freq: float32 [2], replicated, may hold values from 0.6 to 1.6
- boundary_rows: int32 [32768], P(('region', 'sub')), may hold values from 0 to 511
- connectivity: int32 [4, 131072], P(None, ('region', 'sub')), may hold values from 0 to 639
- stress_coef: float32 [4, 131072], P(None, ('region', 'sub')), may hold values from -3 to 3
Outputs:
- stress_psd: float32 [2, 131072], P(None, ('region', 'sub'))
Inputs may be any that keep to these rules, and one draw needn't show every extreme that they name: `boundary_rows`: local row numbers of the sending device. `connectivity`: rows of the node table of the element's device.
All inputs are finite; a program needn't handle non-finite values.
Results may differ from a plain program's by a relative error of at most 0.0013.
Values may be sent and summed in bfloat16 or wider, within the bound.
A program may use at most 64 MiB of HBM per device.

v0:
```python
import jax
import jax.numpy as jnp
from jax import lax
from jax.sharding import PartitionSpec as P


def extended(cells, sides, width):
    for axis, dim in sides:
        count = lax.axis_size(axis)
        ends = count - 1
        head = lax.slice_in_dim(cells, 0, width, axis=dim)
        tail = lax.slice_in_dim(cells, cells.shape[dim] - width, cells.shape[dim], axis=dim)
        cells = jnp.concatenate(
            [
                lax.ppermute(tail, axis, [(i, (i + 1) % count) for i in range(ends)]),
                cells,
                lax.ppermute(head, axis, [((i + 1) % count, i) for i in range(ends)]),
            ],
            axis=dim,
        )
    return cells


def modal_gain(mode_freq, mode_damping, line_omega):
    detune = mode_freq * mode_freq - line_omega * line_omega
    damped = 2.0 * mode_damping * mode_freq * line_omega
    magnitude = detune * detune + damped * damped
    return (detune / magnitude, -damped / magnitude)


def apply_gain(summed, gain_real, gain_imag):
    half_cols = summed.shape[1] // 2
    forced_real = summed[:, :half_cols]
    forced_imag = summed[:, half_cols:]
    out_real = gain_real[:, None] * forced_real - gain_imag[:, None] * forced_imag
    out_imag = gain_real[:, None] * forced_imag + gain_imag[:, None] * forced_real
    return jnp.concatenate([out_real, out_imag], axis=1).astype(jnp.bfloat16)


def scale_lines(summed, mode_freq, mode_damping, line_freq, columns):
    pieces = []
    for line_no in range(line_freq.shape[0]):
        gain_real, gain_imag = modal_gain(mode_freq, mode_damping, line_freq[line_no])
        pieces.append(
            apply_gain(summed[:, line_no * columns : (line_no + 1) * columns], gain_real, gain_imag)
        )
    return jnp.concatenate(pieces, axis=1)


def local(
    mode_rows,
    input_rows,
    input_factor,
    mode_freq,
    mode_damping,
    line_freq,
    boundary_rows,
    connectivity,
    stress_coef,
):
    mode_count = input_rows.shape[1]
    line_count = line_freq.shape[0]
    width_all = input_factor.shape[1]
    columns = width_all // line_count
    partial_value = lax.dot_general(
        input_rows, input_factor, (((0,), (0,)), ((), ())), preferred_element_type=jnp.float32
    )
    summed = lax.psum(
        partial_value.reshape(mode_count // 2, 2 * width_all), ("region", "sub")
    ).reshape(mode_count, width_all)
    pseudo = scale_lines(summed, mode_freq, mode_damping, line_freq, columns)
    responses = jnp.dot(mode_rows, pseudo, preferred_element_type=jnp.float32).astype(jnp.bfloat16)
    rim_rows = boundary_rows.shape[0] // 2
    export = responses[boundary_rows]
    padded = extended(export, ((("region", "sub"), 0),), rim_rows)
    node_table = jnp.concatenate([padded[:rim_rows], responses, padded[3 * rim_rows :]], axis=0)
    stress = stress_coef[0][:, None] * node_table[connectivity[0]].astype(jnp.float32)
    for corner in range(1, connectivity.shape[0]):
        stress = stress + stress_coef[corner][:, None] * node_table[connectivity[corner]].astype(
            jnp.float32
        )
    squares = stress * stress
    power = jnp.stack(
        [
            jnp.mean(squares[:, line_no * columns : (line_no + 1) * columns], axis=1)
            for line_no in range(line_count)
        ],
        axis=0,
    )
    return power


def solution(mesh):
    placed = (
        P(("region", "sub"), None),
        P(("region", "sub"), None),
        P(("region", "sub"), None),
        P(),
        P(),
        P(),
        P(("region", "sub")),
        P(None, ("region", "sub")),
        P(None, ("region", "sub")),
    )
    return jax.shard_map(
        local, mesh=mesh, in_specs=placed, out_specs=P(None, ("region", "sub")), check_vma=False
    )
```

profile of v0, /device:TPU:24, one launch (start us, length us, event | category | flops | bytes accessed | tf_op | source)
XLA Modules:
  0.0 312.2 jit_solution(9872141562445316333)
XLA Ops:
  6.5 0.0 copy-start
  6.6 0.0 all-reduce.2.cloned.1.call-start
  6.6 0.6 copy-done
  7.3 2.4 fusion.14
  9.7 0.0 all-reduce.2.cloned.1.call-update
  9.7 0.6 fusion.13
  10.3 0.0 copy-done.6
  12.8 0.0 copy-done.3
  12.9 0.0 copy-done.4
  12.9 0.0 copy-done.1
  12.9 0.0 copy-done.2
  12.9 1.2 fusion.9
  14.2 262.5 %all-reduce.2.cloned.1.call-done = f32[4096,128]{0,1:T(8,128)} async-done(((f32[4096,128]{0,1:T(8,128)}), f32[4096,128]{0,1:T(8,128)}) %all-reduce.2.cloned.1.call-update) | async-done | bytes 2097168 | tf_op jit(solution)/shard_map/psum | solution.py:68
  276.7 1.8 subtract_convert_fusion.1
  278.5 3.7 %fusion = bf16[512,128]{0,1:T(8,128)(2,1)S(1)} fusion(bf16[512,4096]{1,0:T(8,128)(2,1)} %param.9, bf16[4096,32]{0,1:T(8,128)(2,1)S(1)} %get-tuple-element.11, bf16[4096,32]{0,1:T(8,128)(2,1)S(1)} %get-tuple-element.12, bf16[4096,32]{0,1:T(8,128)(2,1)S(1)} %get-tuple-element.8, bf16[4096,32]{0,1:T(8,128)(2,1)S(1)} %get-tuple-element.7), kind=kOutput, calls=%fused_computation.6 | convolution fusion | flops 541130752 | bytes 5373952 | tf_op jit(solution)/shard_map/dot_general | solution.py:72
  282.2 0.1 copy.25
  282.3 0.7 gather_fusion
  283.0 0.1 copy.34
  283.1 5.7 %collective-permute-start.1 = (bf16[64,128]{0,1:T(8,128)(2,1)S(1)}, bf16[64,128]{0,1:T(8,128)(2,1)S(1)}, u32[]{:S(2)}, u32[]{:S(2)}) collective-permute-start(bf16[64,128]{0,1:T(8,128)(2,1)S(1)} %copy.34), channel_id=1, source_target_pairs={{1,0},{2,1},{3,2},{4,3},{5,4},{6,5},{7,6},{8,7},{9,8},{10,9},{11,1... | collective-permute-start | bytes 49160 | tf_op jit(solution)/shard_map/ppermute | solution.py:17
  288.8 0.1 copy.33
  289.0 1.9 collective-permute-start
  290.9 0.0 collective-permute-done.1
  290.9 7.5 %collective-permute-done = bf16[64,128]{0,1:T(8,128)(2,1)S(1)} collective-permute-done((bf16[64,128]{0,1:T(8,128)(2,1)S(1)}, bf16[64,128]{0,1:T(8,128)(2,1)S(1)}, u32[]{:S(2)}, u32[]{:S(2)}) %collective-permute-start) | collective-permute-done | bytes 16416 | tf_op jit(solution)/shard_map/ppermute | solution.py:15
  298.4 0.1 pad_maximum_fusion
  298.5 0.2 copy.28
  298.7 1.3 gather_fusion.4
  300.1 1.3 gather_fusion.3
  301.4 1.3 gather_fusion.2
  302.7 1.3 gather_fusion.1
  304.1 0.3 add_multiply_fusion
  304.4 0.3 slice_reduce_fusion.1
  304.8 0.6 pad_maximum_fusion.1
  (17 shorter events, 0.1 us)
Async XLA Ops:
  6.5 0.7 copy-start
  6.5 3.2 %copy-start.5 = (f32[2]{0:T(128)S(1)}, f32[2]{0:T(128)}, u32[]{:S(2)}) copy-start(f32[2]{0:T(128)} %param.14) | copy-start | bytes 28
  6.5 3.8 %copy-start.6 = (s32[128]{0:T(128)S(1)}, s32[128]{0:T(128)}, u32[]{:S(2)}) copy-start(s32[128]{0:T(128)} %param.15) | copy-start | bytes 1540
  6.5 6.2 %copy-start.3 = (s32[4,512]{1,0:T(4,128)S(1)}, s32[4,512]{1,0:T(4,128)}, u32[]{:S(2)}) copy-start(s32[4,512]{1,0:T(4,128)} %param.16) | copy-start | bytes 24580
  6.5 6.3 %copy-start.4 = (f32[4,512]{1,0:T(4,128)S(1)}, f32[4,512]{1,0:T(4,128)}, u32[]{:S(2)}) copy-start(f32[4,512]{1,0:T(4,128)} %param.17) | copy-start | bytes 24580
  6.5 6.3 %copy-start.1 = (f32[4096]{0:T(1024)S(1)}, f32[4096]{0:T(1024)}, u32[]{:S(2)}) copy-start(f32[4096]{0:T(1024)} %param.12) | copy-start | bytes 49156
  6.6 6.3 %copy-start.2 = (f32[4096]{0:T(1024)S(1)}, f32[4096]{0:T(1024)}, u32[]{:S(2)}) copy-start(f32[4096]{0:T(1024)} %param.13) | copy-start | bytes 49156
  6.6 270.1 %all-reduce.2.cloned.1.call-start = ((), (), s32[]{:S(2)}) async-start(), calls=%async_computation | async-start | bytes 4194304 | tf_op jit(solution)/shard_map/psum | solution.py:68
  283.1 7.8 %collective-permute-start.1 = (bf16[64,128]{0,1:T(8,128)(2,1)S(1)}, bf16[64,128]{0,1:T(8,128)(2,1)S(1)}, u32[]{:S(2)}, u32[]{:S(2)}) collective-permute-start(bf16[64,128]{0,1:T(8,128)(2,1)S(1)} %copy.34), channel_id=1, source_target_pairs={{1,0},{2,1},{3,2},{4,3},{5,4},{6,5},{7,6},{8,7},{9,8},{10,9},{11,1... | collective-permute-start | bytes 49160 | tf_op jit(solution)/shard_map/ppermute | solution.py:17
  289.0 9.5 %collective-permute-start = (bf16[64,128]{0,1:T(8,128)(2,1)S(1)}, bf16[64,128]{0,1:T(8,128)(2,1)S(1)}, u32[]{:S(2)}, u32[]{:S(2)}) collective-permute-start(bf16[64,128]{0,1:T(8,128)(2,1)S(1)} %copy.33), channel_id=1, source_target_pairs={{0,1},{1,2},{2,3},{3,4},{4,5},{5,6},{6,7},{7,8},{8,9},{9,10},{10,1... | collective-permute-start | bytes 49160 | tf_op jit(solution)/shard_map/ppermute | solution.py:15
Sparse Core Ops, SparseCore 0:
  12.8 263.8 all-reduce.1
where the time goes:
time: 313 us; the launch traced here: 312 us
  waiting for transfers between devices  270 us (86%)
  between operations  16.1 us (5%)
  local copies, waits for them, and re-layouts  7.86 us (3%)
  starting transfers between devices  7.65 us (2%)
  matrix products  6.16 us (2%)
  other arithmetic  4.44 us (1%)
    psum x1, waiting for transfers between devices, local(): lax.psum(partial_value.reshape(mode_count // 2, 2 * width_all), ('region'...  263 us
    ppermute x1, waiting for transfers between devices, extended(): lax.ppermute(tail, axis, [(i, (i + 1) % count) for i in range(ends)])  7.5 us
  transfers between devices with their start and end apart: 3, of which 2 were waited for; matrix products, arithmetic and copies ran while one was open for 1% of the time, Pallas kernels for 0%

commit v1 on v0

--- a/solution.py
+++ b/solution.py
@@ -2,6 +2,7 @@
 import jax.numpy as jnp
 from jax import lax
 from jax.sharding import PartitionSpec as P
+from jax.lax import psum
 
 
 def extended(cells, sides, width):
@@ -65,9 +66,10 @@
     partial_value = lax.dot_general(
         input_rows, input_factor, (((0,), (0,)), ((), ())), preferred_element_type=jnp.float32
     )
-    summed = lax.psum(
-        partial_value.reshape(mode_count // 2, 2 * width_all), ("region", "sub")
-    ).reshape(mode_count, width_all)
+    tell_sections = lambda own_rows: psum(psum(own_rows, "sub"), "region")
+    summed = tell_sections(partial_value.reshape(mode_count // 2, 2 * width_all)).reshape(
+        mode_count, width_all
+    )
     pseudo = scale_lines(summed, mode_freq, mode_damping, line_freq, columns)
     responses = jnp.dot(mode_rows, pseudo, preferred_element_type=jnp.float32).astype(jnp.bfloat16)
     rim_rows = boundary_rows.shape[0] // 2

time: 313 us -> 272 us (0.87)
  waiting for transfers between devices: 270 us -> 228 us
  local copies, waits for them, and re-layouts: 7.86 us -> 13.7 us
  starting transfers between devices: 7.65 us -> 4.37 us
    psum x1 -> x2, waiting for transfers between devices: 263 us -> 221 us  [local(): tell_sections = lambda own_rows: psum(psum(own_rows, 'sub'), 'region')]
    reshape x0 -> x3, local copies, waits for them, and re-layouts: none -> 5.12 us  [the longest x2 3.49 us: local(): tell_sections(partial_value.reshape(mode_count // 2, 2 * width_all))]
    ppermute x1, starting transfers between devices: 5.69 us -> 2.29 us  [extended(): lax.ppermute(head, axis, [((i + 1) % count, i) for i in range(ends)])]
  transfers between devices with their start and end apart: 3 -> 4, of which waited for: 2 -> 3; matrix products, arithmetic and copies ran while one was open for 1% -> 1% of each run, Pallas kernels for 0% -> 0%
where the time goes in v1:
time: 272 us; the launch traced here: 271 us
  waiting for transfers between devices  228 us (84%)
  between operations  16.1 us (6%)
  local copies, waits for them, and re-layouts  13.7 us (5%)
  matrix products  4.9 us (2%)
  other arithmetic  4.43 us (2%)
  starting transfers between devices  4.37 us (2%)
    psum x2, waiting for transfers between devices, local(): tell_sections = lambda own_rows: psum(psum(own_rows, 'sub'), 'region')  221 us
    ppermute x1, waiting for transfers between devices, extended(): lax.ppermute(tail, axis, [(i, (i + 1) % count) for i in range(ends)])  7.38 us
  transfers between devices with their start and end apart: 4, of which 3 were waited for; matrix products, arithmetic and copies ran while one was open for 1% of the time, Pallas kernels for 0%

profile of v1, /device:TPU:24, one launch (start us, length us, event | category | flops | bytes accessed | tf_op | source)
XLA Modules:
  0.0 271.4 jit_solution(16166180158244890134)
XLA Ops:
  6.5 0.7 copy-done
  7.3 1.2 fusion.14
  8.4 1.6 reshape.144
  10.1 0.0 all-reduce.3.cloned.1.call-update
  10.1 0.0 all-reduce.5.cloned.1.call-start
  10.1 73.6 %all-reduce.3.cloned.1.call-done = f32[2048,256]{1,0:T(8,128)} async-done(((f32[2048,256]{1,0:T(8,128)}), f32[2048,256]{1,0:T(8,128)}) %all-reduce.3.cloned.1.call-update) | async-done | bytes 2097168 | tf_op jit(solution)/shard_map/psum | solution.py:69
  83.7 1.6 reshape.145
  85.4 1.9 copy.31
  87.2 0.0 copy-start.1
  87.3 0.0 all-reduce.5.cloned.1.call-update
  87.3 0.6 copy-done.5
  87.9 0.6 fusion.13
  91.1 1.2 fusion.9
  92.3 147.0 %all-reduce.5.cloned.1.call-done = f32[4096,128]{0,1:T(8,128)} async-done(((f32[4096,128]{0,1:T(8,128)}), f32[4096,128]{0,1:T(8,128)}) %all-reduce.5.cloned.1.call-update) | async-done | bytes 2097168 | tf_op jit(solution)/shard_map/psum | solution.py:69
  239.3 1.8 subtract_convert_fusion.1
  241.1 3.7 %fusion = bf16[512,128]{0,1:T(8,128)(2,1)S(1)} fusion(bf16[512,4096]{1,0:T(8,128)(2,1)} %param.9, bf16[4096,32]{0,1:T(8,128)(2,1)S(1)} %get-tuple-element.11, bf16[4096,32]{0,1:T(8,128)(2,1)S(1)} %get-tuple-element.12, bf16[4096,32]{0,1:T(8,128)(2,1)S(1)} %get-tuple-element.8, bf16[4096,32]{0,1:T(8,128)(2,1)S(1)} %get-tuple-element.7), kind=kOutput, calls=%fused_computation.6 | convolution fusion | flops 541130752 | bytes 5373952 | tf_op jit(solution)/shard_map/dot_general | solution.py:74
  244.8 0.1 copy.32
  244.9 0.7 gather_fusion
  245.7 0.1 copy.40
  245.8 2.3 collective-permute-start.1
  248.1 0.1 copy.39
  248.2 2.0 collective-permute-start
  250.3 7.4 %collective-permute-done = bf16[64,128]{0,1:T(8,128)(2,1)S(1)} collective-permute-done((bf16[64,128]{0,1:T(8,128)(2,1)S(1)}, bf16[64,128]{0,1:T(8,128)(2,1)S(1)}, u32[]{:S(2)}, u32[]{:S(2)}) %collective-permute-start) | collective-permute-done | bytes 16416 | tf_op jit(solution)/shard_map/ppermute | solution.py:16
  257.6 0.1 pad_maximum_fusion
  257.8 0.2 copy.35
  257.9 1.3 gather_fusion.4
  259.3 1.3 gather_fusion.3
  260.6 1.3 gather_fusion.2
  262.0 1.3 gather_fusion.1
  263.3 0.3 add_multiply_fusion
  263.7 0.3 slice_reduce_fusion.1
  264.0 0.6 pad_maximum_fusion.1
  (23 shorter events, 0.1 us)
Async XLA Ops:
  6.5 0.7 copy-start
  6.5 77.2 %all-reduce.3.cloned.1.call-start = ((), (), s32[]{:S(2)}) async-start(), calls=%async_computation | async-start | bytes 4194304 | tf_op jit(solution)/shard_map/psum | solution.py:69
  10.1 229.2 %all-reduce.5.cloned.1.call-start = ((), (), s32[]{:S(2)}) async-start(), calls=%async_computation.1 | async-start | bytes 4194304 | tf_op jit(solution)/shard_map/psum | solution.py:69
  87.2 0.7 copy-start.5
  87.2 3.7 %copy-start.6 = (s32[128]{0:T(128)S(1)}, s32[128]{0:T(128)}, u32[]{:S(2)}) copy-start(s32[128]{0:T(128)} %param.15) | copy-start | bytes 1540
  87.2 3.7 %copy-start.3 = (s32[4,512]{1,0:T(4,128)S(1)}, s32[4,512]{1,0:T(4,128)}, u32[]{:S(2)}) copy-start(s32[4,512]{1,0:T(4,128)} %param.16) | copy-start | bytes 24580
  87.2 3.8 %copy-start.4 = (f32[4,512]{1,0:T(4,128)S(1)}, f32[4,512]{1,0:T(4,128)}, u32[]{:S(2)}) copy-start(f32[4,512]{1,0:T(4,128)} %param.17) | copy-start | bytes 24580
  87.2 3.8 %copy-start.1 = (f32[4096]{0:T(1024)S(1)}, f32[4096]{0:T(1024)}, u32[]{:S(2)}) copy-start(f32[4096]{0:T(1024)} %param.12) | copy-start | bytes 49156
  87.2 3.8 %copy-start.2 = (f32[4096]{0:T(1024)S(1)}, f32[4096]{0:T(1024)}, u32[]{:S(2)}) copy-start(f32[4096]{0:T(1024)} %param.13) | copy-start | bytes 49156
  245.8 4.5 %collective-permute-start.1 = (bf16[64,128]{0,1:T(8,128)(2,1)S(1)}, bf16[64,128]{0,1:T(8,128)(2,1)S(1)}, u32[]{:S(2)}, u32[]{:S(2)}) collective-permute-start(bf16[64,128]{0,1:T(8,128)(2,1)S(1)} %copy.40), channel_id=1, source_target_pairs={{1,0},{2,1},{3,2},{4,3},{5,4},{6,5},{7,6},{8,7},{9,8},{10,9},{11,1... | collective-permute-start | bytes 49160 | tf_op jit(solution)/shard_map/ppermute | solution.py:18
  248.2 9.5 %collective-permute-start = (bf16[64,128]{0,1:T(8,128)(2,1)S(1)}, bf16[64,128]{0,1:T(8,128)(2,1)S(1)}, u32[]{:S(2)}, u32[]{:S(2)}) collective-permute-start(bf16[64,128]{0,1:T(8,128)(2,1)S(1)} %copy.39), channel_id=1, source_target_pairs={{0,1},{1,2},{2,3},{3,4},{4,5},{5,6},{6,7},{7,8},{8,9},{9,10},{10,1... | collective-permute-start | bytes 49160 | tf_op jit(solution)/shard_map/ppermute | solution.py:16
Sparse Core Ops, SparseCore 0:
  10.2 73.4 all-reduce.2
  87.4 151.8 all-reduce.4
